TPU v7x, 32 devices: a whole 2x2x4 slice. The times are simulated.
32 devices in a mesh: bins: 16 (over z, y, x), params: 2 (over core).
Axes of the slice: x: 2, y: 2, z: 4, core: 2. Of those that a mesh axis runs over, the one named last changes fastest.
Arguments:
- event_bins: int32 [49152], P('bins'), may hold values from 0 to 16383, as said below
- event_weights: bfloat16 [49152, 3072], P('bins', 'params'), may hold values from -6 to 6
- nominal: bfloat16 [49152], P('bins'), may hold values from 0.5 to 2
- background: float32 [16384], P('bins'), may hold values from 1 to 10
- observed: float32 [16384], P('bins'), may hold values from 1 to 100
Outputs:
- hessian: float32 [3072, 3072], P(('params', 'bins'))
Inputs may be any that keep to these rules, and one draw needn't show every extreme that they name: `event_bins`: each index of bins holds 3072 consecutive events in ascending bin order. The owner of bin b is b // 1024; each owner's bins receive from one index of bins between 96 and 288 of its events, and in every draw every index of bins has some owner that receives exactly 288 of its events.
All inputs are finite; a program needn't handle non-finite values.
Results may differ from a plain program's by a relative error of at most 0.0016.
Values may be sent and summed in bfloat16 or wider, within the bound.
A program may use at most 128 MiB of HBM per device.

v0:
```python
import functools
import math

import jax
import jax.numpy as jnp
from jax import lax
from jax.experimental import pallas as pl
from jax.experimental.pallas import tpu as pltpu
from jax.sharding import PartitionSpec as P


ALIGN = 8
MESH = pl.DeviceIdType.MESH


def from_behind(value, axis, steps):
    count = lax.axis_size(axis)
    pairs = [(source, (source + steps) % count) for source in range(count)]
    return lax.ppermute(value, axis, pairs)


def pack_kernel(owners, slot, first, width, starts_ref, rows_ref, out_ref, held, in_sems, out_sems):
    def fetch(o):
        start = pl.multiple_of(starts_ref[o] * ALIGN, ALIGN)
        return pltpu.make_async_copy(
            rows_ref.at[pl.ds(start, slot), pl.ds(first, width)], held.at[o], in_sems.at[o]
        )

    def store(o):
        return pltpu.make_async_copy(held.at[o], out_ref.at[o], out_sems.at[o])

    @pl.loop(0, owners)
    def _(o):
        fetch(o).start()

    @pl.loop(0, owners)
    def _(o):
        fetch(o).wait()
        store(o).start()

    @pl.loop(0, owners)
    def _(o):
        store(o).wait()


def pack(starts, rows, slot, first, width):
    owners = starts.shape[0]
    return pl.pallas_call(
        functools.partial(pack_kernel, owners, slot, first, width),
        out_shape=jax.ShapeDtypeStruct((owners, slot, width), rows.dtype),
        in_specs=[
            pl.BlockSpec(memory_space=pltpu.SMEM),
            pl.BlockSpec(memory_space=pl.ANY),
        ],
        out_specs=pl.BlockSpec(memory_space=pl.ANY),
        scratch_shapes=[
            pltpu.VMEM((owners, slot, width), rows.dtype),
            pltpu.SemaphoreType.DMA((owners,)),
            pltpu.SemaphoreType.DMA((owners,)),
        ],
        compiler_params=pltpu.CompilerParams(vmem_limit_bytes=32 << 20),
        cost_estimate=pl.CostEstimate(
            flops=0, bytes_accessed=4 * owners * slot * width, transcendentals=0
        ),
        name="pack",
    )(starts, rows)


def meta_kernel(bins_dev, starts_ref, table_ref, out_ref):
    owners, _, slot = out_ref.shape
    events = table_ref.shape[1]
    table = table_ref[...]

    @pl.loop(0, owners)
    def _(o):
        start = starts_ref[o] * ALIGN
        turned = pltpu.roll(table, lax.rem(events - start, events), axis=1)[:, :slot]
        bins = turned[0:1] - (o * bins_dev).astype(jnp.float32)
        inside = (bins >= 0) & (bins < bins_dev)
        out_ref[o, 0:1, :] = jnp.where(inside, bins, -1.0)
        out_ref[o, 1:2, :] = turned[1:2]


def pack_meta(starts, table, slot, bins_dev):
    owners = starts.shape[0]
    return pl.pallas_call(
        functools.partial(meta_kernel, bins_dev),
        out_shape=jax.ShapeDtypeStruct((owners, 2, slot), jnp.float32),
        in_specs=[
            pl.BlockSpec(memory_space=pltpu.SMEM),
            pl.BlockSpec(memory_space=pltpu.VMEM),
        ],
        out_specs=pl.BlockSpec(memory_space=pltpu.VMEM),
        name="pack_meta",
    )(starts, table)


def hist_kernel(chunk, tile, local_ref, rows_ref, out_ref, hot):
    bins, total = hot.shape

    @pl.when(pl.program_id(0) == 0)
    def _():
        ids = lax.broadcasted_iota(jnp.int32, (bins, chunk), 0)

        @pl.loop(0, total // chunk)
        def _(k):
            part = pl.ds(pl.multiple_of(k * chunk, chunk), chunk)
            hot[:, part] = (ids == local_ref[:, part]).astype(jnp.bfloat16)

    @pl.loop(0, bins // tile)
    def _(m):
        part = pl.ds(pl.multiple_of(m * tile, tile), tile)
        out_ref[part, :] = jnp.dot(
            hot[part, :], rows_ref[...], preferred_element_type=jnp.float32
        ).astype(out_ref.dtype)


def histogram_of(local, rows, bins, block, dtype):
    total, width = rows.shape
    return pl.pallas_call(
        functools.partial(hist_kernel, math.gcd(total, 128), math.gcd(bins, 256)),
        grid=(width // block,),
        out_shape=jax.ShapeDtypeStruct((bins, width), dtype),
        in_specs=[
            pl.BlockSpec((1, total), lambda j: (0, 0)),
            pl.BlockSpec((total, block), lambda j: (0, j)),
        ],
        out_specs=pl.BlockSpec((bins, block), lambda j: (0, j)),
        scratch_shapes=[pltpu.VMEM((bins, total), jnp.bfloat16)],
        compiler_params=pltpu.CompilerParams(
            vmem_limit_bytes=40 << 20, dimension_semantics=("arbitrary",)
        ),
        cost_estimate=pl.CostEstimate(
            flops=2 * bins * total * width, bytes_accessed=2 * total * width, transcendentals=0
        ),
        name="histogram",
    )(local, rows)


def reduce_kernel(
    piece, shares_ref, out_ref, own, got_near, sums, got_far,
    own_sem, near_send, near_recv, far_send, far_recv,
):
    far, near, rows, _ = shares_ref.shape
    me = lax.axis_index("bins")
    f, n = me // near, lax.rem(me, near)

    def near_peer(d):
        return lax.rem(n + d, near)

    def far_peer(d):
        return lax.rem(f + d, far)

    barrier = pltpu.get_barrier_semaphore()
    for d in range(1, near):
        pl.semaphore_signal(
            barrier, inc=1, device_id={"bins": f * near + near_peer(d)}, device_id_type=MESH
        )
    for d in range(1, far):
        pl.semaphore_signal(
            barrier, inc=1, device_id={"bins": far_peer(d) * near + n}, device_id_type=MESH
        )
    pl.semaphore_wait(barrier, near + far - 2)

    def part_of(c):
        return pl.ds(pl.multiple_of(c * piece, piece), piece)

    def near_copy(d, c):
        return pltpu.make_async_remote_copy(
            src_ref=shares_ref.at[:, near_peer(d), part_of(c), :],
            dst_ref=got_near.at[d - 1, :, part_of(c), :],
            send_sem=near_send.at[d - 1, c],
            recv_sem=near_recv.at[d - 1, c],
            device_id={"bins": f * near + near_peer(d)},
            device_id_type=MESH,
        )

    def far_copy(d, c):
        return pltpu.make_async_remote_copy(
            src_ref=sums.at[far_peer(d), part_of(c), :],
            dst_ref=got_far.at[d - 1, part_of(c), :],
            send_sem=far_send.at[d - 1, c],
            recv_sem=far_recv.at[d - 1, c],
            device_id={"bins": far_peer(d) * near + n},
            device_id_type=MESH,
        )

    own_copy = pltpu.make_async_copy(shares_ref.at[:, n], own, own_sem)
    own_copy.start()
    pieces = rows // piece

    @pl.loop(0, pieces)
    def _(c):
        for d in range(1, near):
            near_copy(d, c).start()

    own_copy.wait()

    @pl.loop(0, pieces)
    def _(c):
        part = part_of(c)
        for d in range(1, near):
            near_copy(d, c).wait_recv()

        @pl.loop(0, far)
        def _(k):
            total = own[k, part, :].astype(jnp.float32)
            for d in range(1, near):
                total += got_near[d - 1, k, part, :].astype(jnp.float32)
            sums[k, part, :] = total

        for d in range(1, far):
            far_copy(d, c).start()

    @pl.loop(0, pieces)
    def _(c):
        part = part_of(c)
        for d in range(1, far):
            far_copy(d, c).wait_recv()
        total = sums[f, part, :]
        for d in range(1, far):
            total += got_far[d - 1, part, :]
        out_ref[part, :] = total
        for d in range(1, near):
            near_copy(d, c).wait_send()
        for d in range(1, far):
            far_copy(d, c).wait_send()


def reduce_shares(shares):
    owners, rows, cols = shares.shape
    near = math.isqrt(owners)
    while owners % near:
        near -= 1
    far = owners // near
    piece = 16 if rows % 16 == 0 else rows
    pieces = rows // piece
    return pl.pallas_call(
        functools.partial(reduce_kernel, piece),
        out_shape=jax.ShapeDtypeStruct((rows, cols), jnp.float32),
        in_specs=[pl.BlockSpec(memory_space=pl.ANY)],
        out_specs=pl.BlockSpec(memory_space=pltpu.VMEM),
        scratch_shapes=[
            pltpu.VMEM((far, rows, cols), shares.dtype),
            pltpu.VMEM((near - 1, far, rows, cols), shares.dtype),
            pltpu.VMEM((far, rows, cols), jnp.float32),
            pltpu.VMEM((far - 1, rows, cols), jnp.float32),
            pltpu.SemaphoreType.DMA,
            pltpu.SemaphoreType.DMA((near - 1, pieces)),
            pltpu.SemaphoreType.DMA((near - 1, pieces)),
            pltpu.SemaphoreType.DMA((far - 1, pieces)),
            pltpu.SemaphoreType.DMA((far - 1, pieces)),
        ],
        compiler_params=pltpu.CompilerParams(
            collective_id=1, has_side_effects=True, vmem_limit_bytes=40 << 20
        ),
        name="reduce_shares",
    )(shares.reshape(far, near, rows, cols))


def body(event_bins, event_weights, nominal, background, observed):
    owners = lax.axis_size("bins")
    groups_count = lax.axis_size("params")
    events = event_bins.shape[0]
    width_g = event_weights.shape[1]
    bins_dev = background.shape[0]
    capacity = 3 * events // (2 * owners)
    slot = -(-capacity // ALIGN) * ALIGN + ALIGN
    chunks = 2 if width_g % 512 == 0 else 1
    width = width_g // chunks
    block = math.gcd(width, 256)

    destination = event_bins // bins_dev
    targets = jnp.arange(owners, dtype=jnp.int32)
    before = jnp.sum((destination[None, :] < targets[:, None]).astype(jnp.int32), axis=1)
    starts = jnp.minimum(before // ALIGN, (events - slot) // ALIGN)

    table = jnp.stack([event_bins.astype(jnp.float32), nominal.astype(jnp.float32)])
    table = jnp.concatenate([table, jnp.zeros((6, events), jnp.float32)], axis=0)
    meta = pack_meta(starts, table, slot, bins_dev)
    got_meta = lax.all_to_all(meta, "bins", split_axis=0, concat_axis=0, tiled=True)
    local = got_meta[:, 0].astype(jnp.int32).reshape(1, owners * slot)
    got_nominal = got_meta[:, 1].astype(jnp.bfloat16).reshape(owners * slot, 1)
    got_nominal = jnp.broadcast_to(got_nominal, (owners * slot, 128))
    nominal_sum = histogram_of(local, got_nominal, bins_dev, 128, jnp.float32)[:, 0]
    yields = background + nominal_sum
    curvature = observed / (yields * yields)

    parts = []
    for c in range(chunks):
        packed = pack(starts, event_weights, slot, c * width, width)
        got = lax.all_to_all(packed, "bins", split_axis=0, concat_axis=0, tiled=True)
        got = got.reshape(owners * slot, width)
        parts.append(histogram_of(local, got, bins_dev, block, jnp.bfloat16))
    templates = jnp.concatenate(parts, axis=1)
    weighted = (curvature[:, None] * templates.astype(jnp.float32)).astype(jnp.bfloat16)
    pieces = [templates]
    for shift_by in range(1, groups_count // 2 + 1):
        shifted = [from_behind(part, "params", -shift_by) for part in parts]
        pieces.append(jnp.concatenate(shifted, axis=1))
    partners = jnp.concatenate(pieces, axis=1)
    dims = (((0,), (0,)), ((), ()))
    full = lax.dot_general(weighted, partners, dims, preferred_element_type=jnp.float32)
    full = full.astype(jnp.bfloat16)
    shares = full.reshape(owners, width_g // owners, full.shape[1])
    summed = reduce_shares(shares)
    return summed * (1.0 / (bins_dev * owners))


LANES = 128
TILE = 256


def shift(value, pairs):
    return lax.ppermute(value, "bins", pairs)


def xor_of(a, b, count):
    total, bit = 0, 1
    while bit < count:
        total = total + bit * lax.rem(a // bit + b // bit, 2)
        bit *= 2
    return total


def diagonal():
    rows = lax.broadcasted_iota(jnp.int32, (LANES, LANES), 0)
    return rows == lax.broadcasted_iota(jnp.int32, (LANES, LANES), 1)


def slots_kernel(bins_dev, starts_ref, ids_ref, nominal_ref, out_ref):
    owners = starts_ref.shape[0]
    slot = out_ref.shape[1]
    events = ids_ref.shape[1]
    first = lax.broadcasted_iota(jnp.int32, (8, events), 0) == 0
    table = jnp.where(first, ids_ref[...].astype(jnp.float32), nominal_ref[...].astype(jnp.float32))
    lanes = lax.broadcasted_iota(jnp.int32, (1, slot), 1)
    out_ref[pl.ds(2 * owners, 1), :] = jnp.zeros((1, slot), jnp.float32)

    @pl.loop(0, owners)
    def _(o):
        start = starts_ref[o]
        turned = pltpu.roll(table, lax.rem(events - start * 16, events), axis=1)
        bins = turned[0:1, :slot] - (o * bins_dev).astype(jnp.float32)
        inside = (bins >= 0) & (bins < bins_dev)
        out_ref[pl.ds(o, 1), :] = jnp.where(inside, bins, -1.0)
        out_ref[pl.ds(owners + o, 1), :] = turned[1:2, :slot]
        out_ref[pl.ds(2 * owners, 1), :] += jnp.where(lanes == o, start.astype(jnp.float32), 0.0)


def slots_of(starts, ids, nominal, slot, bins_dev):
    owners, events = starts.shape[0], ids.shape[0]
    return pl.pallas_call(
        functools.partial(slots_kernel, bins_dev),
        out_shape=jax.ShapeDtypeStruct((2 * owners + 1, slot), jnp.float32),
        in_specs=[pl.BlockSpec(memory_space=pltpu.SMEM)]
        + [pl.BlockSpec(memory_space=pltpu.VMEM)] * 2,
        out_specs=pl.BlockSpec(memory_space=pltpu.VMEM),
        name="slots",
    )(starts, ids.reshape(1, events), nominal.reshape(1, events))


def chain_kernel(
    near, far, chunks, pieces, slot, starts_ref, local_ref, worth_ref, data_ref, weights_ref, *refs
):
    firsts = refs[:near]
    out_ref, weighted_ref = refs[near : near + 2]
    rows_refs = refs[near + 2 : near + 2 + chunks]
    (
        heads, sums, got_sums, got_data, levels, curve_ref, stage, stage_sem,
        head_sem, head_keep, sums_send, sums_recv, data_send, data_recv,
        window, acc, own, send_q, send_s, got_q, got_s,
        row_sem, row_send, row_recv, q_send, q_recv, s_send, s_recv,
        own_sem, side_send, side_recv, pair_send, pair_recv,
    ) = refs[near + 2 + chunks :]
    owners = near * far
    here = lax.axis_index("bins")
    core = lax.axis_index("params")
    z, me = here // near, lax.rem(here, near)
    bins_dev = own.shape[1] // near
    width = chunks * LANES
    held = near // pieces
    size = held * bins_dev
    direct = [d for d in range(1, near) if near != 4 or d != 3]

    def side(d):
        return z * near + xor_of(me, d, near)

    def along(way):
        return (z + 1 - 2 * way) * near + me

    def peer(k):
        return lax.rem(z + k, far)

    barrier = pltpu.get_barrier_semaphore()
    for d in range(1, near):
        pl.semaphore_signal(barrier, inc=1, device_id={"bins": side(d)}, device_id_type=MESH)
    for k in range(1, far):
        pl.semaphore_signal(
            barrier, inc=1, device_id={"bins": peer(k) * near + me}, device_id_type=MESH
        )
    pl.semaphore_signal(barrier, inc=1, device_id={"params": 1 - core}, device_id_type=MESH)
    pl.semaphore_wait(barrier, near + far - 1)

    events = weights_ref.shape[0]
    ahead = firsts[0].shape[0]
    lower = (z < far // 2).astype(jnp.int32)
    head_start = lower * (events - ahead)
    rest_start = (1 - lower) * ahead

    def quarter(d, c):
        start = xor_of(me, d, near) * width + c * LANES
        return pl.ds(pl.multiple_of(start, LANES), LANES)

    def row_part(c):
        if c > 0:
            return pl.ds(0, events)
        return pl.ds(pl.multiple_of(rest_start, 16), events - ahead)

    def row_copy(c, d):
        return pltpu.make_async_remote_copy(
            src_ref=weights_ref.at[row_part(c), quarter(d, c)],
            dst_ref=rows_refs[c].at[d, row_part(c), :],
            send_sem=row_send.at[c, d],
            recv_sem=row_recv.at[c, d],
            device_id={"bins": side(d)},
            device_id_type=MESH,
        )

    def row_local(c):
        return pltpu.make_async_copy(
            weights_ref.at[row_part(c), quarter(0, c)],
            rows_refs[c].at[0, row_part(c), :],
            row_sem.at[c],
        )

    def head_local(d):
        return pltpu.make_async_copy(firsts[d], heads.at[d], head_sem.at[d])

    def head_stay(d):
        part = pl.ds(pl.multiple_of(head_start, 16), ahead)
        return pltpu.make_async_copy(firsts[d], rows_refs[0].at[d, part, :], head_keep.at[d])

    def sums_copy(k):
        lines_from = pl.ds(pl.multiple_of(peer(k) * curve_ref.shape[0], 8), curve_ref.shape[0])
        return pltpu.make_async_remote_copy(
            src_ref=sums.at[lines_from, :],
            dst_ref=got_sums.at[k - 1],
            send_sem=sums_send.at[k - 1],
            recv_sem=sums_recv.at[k - 1],
            device_id={"bins": peer(k) * near + me},
            device_id_type=MESH,
        )

    def data_copy(d):
        return pltpu.make_async_remote_copy(
            src_ref=data_ref,
            dst_ref=got_data.at[d - 1],
            send_sem=data_send.at[d - 1],
            recv_sem=data_recv.at[d - 1],
            device_id={"bins": side(d)},
            device_id_type=MESH,
        )

    for d in range(near):
        head_local(d).start()
    for d in range(1, near):
        data_copy(d).start()
    for c in range(chunks):
        for d in range(1, near):
            row_copy(c, d).start()
    for c in range(chunks):
        row_local(c).start()
    for d in range(near):
        head_stay(d).start()

    def nominal_sums():
        @pl.loop(0, owners)
        def _(o):
            @pl.loop(0, bins_dev // TILE)
            def _(k):
                bins = k * TILE + lax.broadcasted_iota(jnp.int32, (TILE, near * slot), 0)
                total = jnp.sum(
                    jnp.where(bins == local_ref[o], worth_ref[o], 0.0), axis=1, keepdims=True
                )
                for h in range(TILE // LANES):
                    part = total[h * LANES : (h + 1) * LANES]
                    line = o * (bins_dev // LANES) + k * (TILE // LANES) + h
                    sums[pl.ds(line, 1), :] = jnp.sum(
                        jnp.where(diagonal(), part, 0.0), axis=0, keepdims=True
                    )

        for k in range(1, far):
            sums_copy(k).start()

    def finish_sums():
        own_lines = pl.ds(pl.multiple_of(z * curve_ref.shape[0], 8), curve_ref.shape[0])
        total = sums[own_lines, :]
        for k in range(1, far):
            sums_copy(k).wait_recv()
            total += got_sums[k - 1]
        lines_dev = bins_dev // LANES
        levels[0, pl.ds(pl.multiple_of(me * lines_dev, 8), lines_dev), :] = data_ref[0:lines_dev, :]
        levels[1, pl.ds(pl.multiple_of(me * lines_dev, 8), lines_dev), :] = data_ref[
            lines_dev : 2 * lines_dev, :
        ]
        for d in range(1, near):
            data_copy(d).wait_recv()
            part = pl.ds(pl.multiple_of(xor_of(me, d, near) * lines_dev, 8), lines_dev)
            levels[0, part, :] = got_data[d - 1, 0:lines_dev, :]
            levels[1, part, :] = got_data[d - 1, lines_dev : 2 * lines_dev, :]
        yields = levels[0] + total
        curve_ref[...] = levels[1] / (yields * yields)

    def chain_copies(way, c, r, p):
        return [
            pltpu.make_async_remote_copy(
                src_ref=source.at[way, c, r - 1, p],
                dst_ref=target.at[way, c, r - 1, p],
                send_sem=sent.at[way, c, r - 1, p],
                recv_sem=landed.at[way, c, r - 1, p],
                device_id={"bins": along(way)},
                device_id_type=MESH,
            )
            for source, target, sent, landed in (
                (send_q, got_q, q_send, q_recv), (send_s, got_s, s_send, s_recv)
            )
        ]

    def fold(c, plane, p, inputs, finish, early=False):
        @pl.loop(0, held)
        def _(i):
            owner = plane * near + p * held + i
            for s in range(near):
                start = starts_ref[s * owners + owner]
                if early:
                    start = jnp.maximum(start - lower * ((events - ahead) // 16), 0)
                    part = heads[s, pl.ds(start * 16, slot), :]
                else:
                    part = rows_refs[c][s, pl.ds(start * 16, slot), :]
                window[s * slot : (s + 1) * slot, :] = part

            @pl.loop(0, bins_dev // TILE)
            def _(k):
                bins = k * TILE + lax.broadcasted_iota(jnp.int32, (TILE, near * slot), 0)
                hot = (bins == local_ref[owner]).astype(jnp.bfloat16)
                acc[...] = jnp.dot(hot, window[...], preferred_element_type=jnp.float32)
                base = i * (bins_dev // LANES) + k * (TILE // LANES)
                eye = diagonal()
                for way, r, has in inputs:
                    @pl.when(has)
                    def _():
                        for h in range(TILE // LANES):
                            line = base + h
                            part = pl.ds(pl.multiple_of(line * LANES, LANES), LANES)
                            step = got_s[way, c, r - 1, p, pl.ds(line, 1), :]
                            step = jnp.sum(jnp.where(eye, step, 0.0), axis=1, keepdims=True)
                            coded = got_q[way, c, r - 1, p, part, :].astype(jnp.int32)
                            acc[h * LANES : (h + 1) * LANES, :] += (
                                coded.astype(jnp.float32) * step
                            )
                for h in range(TILE // LANES):
                    line = base + h
                    part = pl.ds(pl.multiple_of(line * LANES, LANES), LANES)
                    finish(acc[h * LANES : (h + 1) * LANES, :], line, part, eye)

    def wait_chain(way, c, r, p):
        for copy in chain_copies(way, c, r, p):
            copy.wait_recv()

    def rounds(c, span, first, last, early=False):
        low, high = span

        @pl.loop(first, last)
        def _(r):
            @pl.loop(low, high)
            def _(p):
                for way in range(2):
                    step_in = z if way == 0 else far - 1 - z

                    @pl.when(step_in < r)
                    def _():
                        inputs = []
                        if first > 1:
                            has = step_in > 0
                            inputs = [(way, r - 1, has)]

                            @pl.when(has)
                            def _():
                                wait_chain(way, c, r - 1, p)

                        def code(value, line, part, eye):
                            most = jnp.max(jnp.abs(value), axis=1, keepdims=True)
                            wide = most * (2.0**23 + 1.0)
                            step = (wide + (most - wide)) * 2.0**-14
                            factor = jnp.where(most > 1e-30, 1.0 / step, 0.0)
                            coded = jnp.round(value * factor).astype(jnp.int32)
                            send_q[way, c, r - 1, p, part, :] = coded.astype(send_q.dtype)
                            send_s[way, c, r - 1, p, pl.ds(line, 1), :] = jnp.sum(
                                jnp.where(eye, step, 0.0), axis=0, keepdims=True
                            )

                        plane = z + (far - r) * (1 - 2 * way)
                        fold(c, plane, p, inputs, code, early)
                        for copy in chain_copies(way, c, r, p):
                            copy.start()

    def rows_part(p):
        return pl.ds(pl.multiple_of(p * size, size), size)

    def side_copy(c, d, p, source=0, hop=None):
        hop = d if hop is None else hop
        origin = own.at[c] if source == 0 else out_ref.at[0, source, c]
        return pltpu.make_async_remote_copy(
            src_ref=origin.at[rows_part(p), :],
            dst_ref=out_ref.at[0, d, c, rows_part(p), :],
            send_sem=side_send.at[c, d, p],
            recv_sem=side_recv.at[c, d, p],
            device_id={"bins": side(hop)},
            device_id_type=MESH,
        )

    def pair_copy(c, d, p):
        source = own.at[c] if d == 0 else out_ref.at[0, d, c]
        return pltpu.make_async_remote_copy(
            src_ref=source.at[rows_part(p), :],
            dst_ref=out_ref.at[1, d, c, rows_part(p), :],
            send_sem=pair_send.at[c, d, p],
            recv_sem=pair_recv.at[c, d, p],
            device_id={"params": 1 - core},
            device_id_type=MESH,
        )

    def keep_copy(c, p):
        return pltpu.make_async_copy(
            own.at[c, rows_part(p), :], out_ref.at[0, 0, c, rows_part(p), :], own_sem.at[c, p]
        )

    def finish(c, p):
        @pl.when(z > 0)
        def _():
            wait_chain(0, c, far - 1, p)

        @pl.when(z < far - 1)
        def _():
            wait_chain(1, c, far - 1, p)

        def store(value, line, part, eye):
            row = pl.ds(pl.multiple_of(p * size + line * LANES, LANES), LANES)
            own[c, row, :] = value.astype(own.dtype)

        fold(c, z, p, [(0, far - 1, z > 0), (1, far - 1, z < far - 1)], store)
        for d in direct:
            side_copy(c, d, p).start()
        pair_copy(c, 0, p).start()
        keep_copy(c, p).start()

    def forward(c, p, act):
        if near == 4:
            @pl.when(lax.rem(p, 2) == 0)
            def _():
                act(side_copy(c, 3, p, 1, 2))

            @pl.when(lax.rem(p, 2) == 1)
            def _():
                act(side_copy(c, 3, p, 2, 1))

    def over(c, span, act):
        @pl.loop(span[0], span[1])
        def _(p):
            act(c, p)

    def relay(c, p):
        for d in direct:
            side_copy(c, d, p).wait_recv()
        forward(c, p, lambda copy: copy.start())
        for d in direct:
            pair_copy(c, d, p).start()

    def relay_last(c, p):
        for d in range(1, near):
            if d not in direct:
                side_copy(c, d, p).wait_recv()
                pair_copy(c, d, p).start()

    def stage_copy(c, d, p):
        return pltpu.make_async_copy(
            out_ref.at[0, d, c, rows_part(p), :], stage.at[p, d - 1], stage_sem.at[p, d - 1]
        )

    def fetch(c, p):
        for d in range(1, near):
            stage_copy(c, d, p).start()

    def weigh(c, p):
        for d in range(1, near):
            stage_copy(c, d, p).wait()
        piece = weighted_ref.shape[0] // near
        depth = 4 * LANES
        rows = lax.broadcasted_iota(jnp.int32, (piece, LANES), 0) + me * piece
        lanes = lax.broadcasted_iota(jnp.int32, (piece, LANES), 1) + c * LANES
        pick = (rows == lanes).astype(jnp.bfloat16)

        @pl.loop(0, size // depth)
        def _(b):
            eye = diagonal()
            curves = []
            for h in range(depth // LANES):
                at = p * (size // LANES) + b * (depth // LANES) + h
                line = curve_ref[pl.ds(at, 1), :]
                curves.append(jnp.sum(jnp.where(eye, line, 0.0), axis=1, keepdims=True))
            curve = jnp.concatenate(curves, axis=0)
            here_part = pl.ds(pl.multiple_of(b * depth, depth), depth)
            part = pl.ds(pl.multiple_of(p * size + b * depth, depth), depth)
            for d in range(near):
                if d == 0:
                    value = own[c, part, :]
                else:
                    value = stage[p, d - 1, here_part, :]
                value = (curve * value.astype(jnp.float32)).astype(jnp.bfloat16)
                picked = lax.dot_general(
                    pick, value, (((1,), (1,)), ((), ())), preferred_element_type=jnp.float32
                ).astype(weighted_ref.dtype)
                block = slice(d * piece, (d + 1) * piece)
                if c == 0:
                    weighted_ref[block, part] = picked
                else:
                    weighted_ref[block, part] += picked

    def weigh_all(c, span):
        over(c, span, relay_last)
        over(c, span, fetch)
        over(c, span, weigh)

    every = (0, pieces)
    groups = [(c, every) for c in range(chunks - 1)]
    groups += [(chunks - 1, (0, pieces // 2)), (chunks - 1, (pieces // 2, pieces))]
    for d in range(near):
        head_local(d).wait()
    for g, (c, span) in enumerate(groups):
        new = g == 0 or groups[g - 1][0] != c
        if new and c > 0:
            row_local(c).wait()
            for d in range(1, near):
                row_copy(c, d).wait_recv()
        rounds(c, span, 1, 2, g == 0)
        if g == 0:
            nominal_sums()
            row_local(0).wait()
            head_stay(0).wait()
            for d in range(1, near):
                head_stay(d).wait()
                row_copy(0, d).wait_recv()
        if g > 0:
            over(*groups[g - 1], finish)
        rounds(c, span, 2, far)
        if g == 0:
            finish_sums()
        if g > 0:
            over(*groups[g - 1], relay)
        if g > 1:
            weigh_all(*groups[g - 2])
    over(*groups[-1], finish)
    weigh_all(*groups[-2])
    over(*groups[-1], relay)
    weigh_all(*groups[-1])

    for k in range(1, far):
        sums_copy(k).wait_send()
    for d in range(1, near):
        data_copy(d).wait_send()
    for c in range(chunks):
        for d in range(1, near):
            row_copy(c, d).wait_send()

        @pl.loop(0, pieces)
        def _(p):
            keep_copy(c, p).wait()
            for d in direct:
                side_copy(c, d, p).wait_send()
            forward(c, p, lambda copy: copy.wait_send())
            for d in range(near):
                pair_copy(c, d, p).wait_send()
                pair_copy(c, d, p).wait_recv()

            @pl.loop(1, far)
            def _(r):
                for way in range(2):
                    step_in = z if way == 0 else far - 1 - z

                    @pl.when(step_in < r)
                    def _():
                        for copy in chain_copies(way, c, r, p):
                            copy.wait_send()


def chain(starts, local, worth, data, weights, firsts, near, far, chunks, slot, bins_dev):
    events = weights.shape[0]
    ahead = firsts[0].shape[0]
    pieces = near
    bins = near * bins_dev
    size = bins // pieces
    hops = (2, chunks, far - 1, pieces)
    lines = bins // LANES
    dma = pltpu.SemaphoreType.DMA
    rows = jnp.bfloat16
    table = jnp.float32
    return pl.pallas_call(
        functools.partial(chain_kernel, near, far, chunks, pieces, slot),
        out_shape=[
            jax.ShapeDtypeStruct((2, near, chunks, bins, LANES), rows),
            jax.ShapeDtypeStruct((chunks * LANES * near // far, bins), rows),
        ],
        in_specs=[pl.BlockSpec(memory_space=pltpu.SMEM)]
        + [pl.BlockSpec(memory_space=pltpu.VMEM)] * 3
        + [pl.BlockSpec(memory_space=pl.ANY)] * (1 + near),
        out_specs=[
            pl.BlockSpec(memory_space=pl.ANY),
            pl.BlockSpec(memory_space=pltpu.VMEM),
        ],
        scratch_shapes=[pltpu.VMEM((near, events, LANES), rows)] * chunks
        + [
            pltpu.VMEM((near, ahead, LANES), rows),
            pltpu.VMEM((far * lines, LANES), table),
            pltpu.VMEM((far - 1, lines, LANES), table),
            pltpu.VMEM((near - 1,) + data.shape, table),
            pltpu.VMEM((2, lines, LANES), table),
            pltpu.VMEM((lines, LANES), table),
            pltpu.VMEM((pieces, near - 1, size, LANES), rows),
            dma((pieces, near - 1)),
            dma((near,)),
            dma((near,)),
            dma((far - 1,)),
            dma((far - 1,)),
            dma((near - 1,)),
            dma((near - 1,)),
            pltpu.VMEM((near * slot, LANES), rows),
            pltpu.VMEM((TILE, LANES), table),
            pltpu.VMEM((chunks, bins, LANES), rows),
            pltpu.VMEM(hops + (size, LANES), jnp.int16),
            pltpu.VMEM(hops + (size // LANES, LANES), table),
            pltpu.VMEM(hops + (size, LANES), jnp.int16),
            pltpu.VMEM(hops + (size // LANES, LANES), table),
            dma((chunks,)),
            dma((chunks, near)),
            dma((chunks, near)),
            dma(hops),
            dma(hops),
            dma(hops),
            dma(hops),
            dma((chunks, pieces)),
            dma((chunks, near, pieces)),
            dma((chunks, near, pieces)),
            dma((chunks, near, pieces)),
            dma((chunks, near, pieces)),
        ],
        compiler_params=pltpu.CompilerParams(
            collective_id=3, has_side_effects=True, vmem_limit_bytes=62 << 20
        ),
        name="chain",
    )(starts, local, worth, data, weights, *firsts)


def tail_kernel(
    near, far, templates_ref, weighted, out_ref, held, total, coded, own, got,
    hand, kept, merged, sems, sends, recvs, hand_recvs,
):
    groups, _, chunks, _, _ = templates_ref.shape
    here = lax.axis_index("bins")
    z, me = here // near, lax.rem(here, near)
    piece = own.shape[0]
    count = groups * near * chunks
    step = 2 * LANES

    def peer(k):
        return lax.rem(z + k, far)

    barrier = pltpu.get_barrier_semaphore()
    for k in range(1, far):
        pl.semaphore_signal(
            barrier, inc=1, device_id={"bins": peer(k) * near + me}, device_id_type=MESH
        )

    def fetch(n):
        part = templates_ref.at[n // (near * chunks), lax.rem(n // chunks, near), lax.rem(n, chunks)]
        return pltpu.make_async_copy(
            part, held.at[:, pl.ds(pl.multiple_of(n * LANES, LANES), LANES)], sems.at[n]
        )

    @pl.loop(0, count)
    def _(n):
        fetch(n).start()

    pl.semaphore_wait(barrier, far - 1)

    def rows_for(target):
        return pl.ds(pl.multiple_of(xor_of(me, target, near) * piece, 16), piece)

    def columns_of(n):
        return pl.ds(pl.multiple_of(n * step, step), step)

    def send(source, target, landed, j, n, to):
        return pltpu.make_async_remote_copy(
            src_ref=source,
            dst_ref=target.at[:, columns_of(n)],
            send_sem=sends.at[j, n],
            recv_sem=landed,
            device_id={"bins": to * near + me},
            device_id_type=MESH,
        )

    half = z // 2
    at_end = (z == 0) | (z == far - 1)
    within = 1 + half
    end = half * (far - 1)

    def to_inner(j, n):
        target = (far - 1 - within, far - 1 - z, within)[j]
        source = coded.at[rows_for(target), columns_of(n)]
        if j == 2:
            return send(source, got.at[half], recvs.at[half, n], j, n, within)
        return send(source, hand.at[j], hand_recvs.at[j, n], j, n, within)

    def from_inner(j, n):
        target = (far - 1 - z, far - 1 - end, end)[j]
        if j == 2:
            source = coded.at[rows_for(target), columns_of(n)]
        else:
            source = merged.at[j, :, columns_of(n)]
        return send(source, got.at[half], recvs.at[half, n], j, n, target)

    def merge(n):
        for j in range(2):
            to_inner(j, n).wait_recv()
            part = kept[j, :, columns_of(n)] + hand[j, :, columns_of(n)].astype(jnp.float32)
            merged[j, :, columns_of(n)] = part.astype(merged.dtype)
            from_inner(j, n).start()

    inner = jnp.logical_not(at_end)
    lag = 2

    @pl.loop(0, count // 2)
    def _(n):
        fetch(2 * n).wait()
        fetch(2 * n + 1).wait()
        total[...] = jnp.dot(
            weighted[...], held[:, columns_of(n)], preferred_element_type=jnp.float32
        )
        coded[:, columns_of(n)] = total[...].astype(coded.dtype)
        own[:, columns_of(n)] = total[rows_for(z), :]

        @pl.when(at_end)
        def _():
            for j in range(3):
                to_inner(j, n).start()

        @pl.when(inner)
        def _():
            from_inner(2, n).start()
            kept[0, :, columns_of(n)] = total[rows_for(far - 1 - z), :]
            kept[1, :, columns_of(n)] = total[rows_for(far - 1 - end), :]

        @pl.when(inner & (n >= lag))
        def _():
            merge(n - lag)

    @pl.when(inner)
    def _():
        @pl.loop(count // 2 - lag, count // 2)
        def _(n):
            merge(n)

    @pl.loop(0, count // 2)
    def _(n):
        for j in range(2):
            send(merged.at[0, :, columns_of(n)], got.at[j], recvs.at[j, n], 0, n, within).wait_recv()
        for side in range(2):
            place = 2 * n + side
            group = place // (near * chunks)
            d = lax.rem(place // chunks, near)
            start = ((group * near + xor_of(me, d, near)) * chunks + lax.rem(place, chunks)) * LANES
            part = pl.ds(pl.multiple_of(place * LANES, LANES), LANES)
            value = own[:, part]
            for j in range(2):
                value += got[j, :, part].astype(jnp.float32)
            out_ref[:, pl.ds(pl.multiple_of(start, LANES), LANES)] = value

    @pl.loop(0, count // 2)
    def _(n):
        for j in range(3):
            @pl.when(at_end)
            def _():
                to_inner(j, n).wait_send()

            @pl.when(inner)
            def _():
                from_inner(j, n).wait_send()


def tail(templates, weighted, near, far):
    groups, _, chunks, bins, _ = templates.shape
    piece = chunks * LANES // far
    columns = groups * near * chunks * LANES
    count = groups * near * chunks
    return pl.pallas_call(
        functools.partial(tail_kernel, near, far),
        out_shape=jax.ShapeDtypeStruct((piece, columns), jnp.float32),
        in_specs=[pl.BlockSpec(memory_space=pl.ANY), pl.BlockSpec(memory_space=pltpu.VMEM)],
        out_specs=pl.BlockSpec(memory_space=pltpu.VMEM),
        scratch_shapes=[
            pltpu.VMEM((bins, columns), jnp.bfloat16),
            pltpu.VMEM((near * piece, 2 * LANES), jnp.float32),
            pltpu.VMEM((near * piece, columns), jnp.bfloat16),
            pltpu.VMEM((piece, columns), jnp.float32),
            pltpu.VMEM((2, piece, columns), jnp.bfloat16),
            pltpu.VMEM((2, piece, columns), jnp.bfloat16),
            pltpu.VMEM((2, piece, columns), jnp.float32),
            pltpu.VMEM((2, piece, columns), jnp.bfloat16),
            pltpu.SemaphoreType.DMA((count,)),
            pltpu.SemaphoreType.DMA((3, count // 2)),
            pltpu.SemaphoreType.DMA((2, count // 2)),
            pltpu.SemaphoreType.DMA((2, count // 2)),
        ],
        compiler_params=pltpu.CompilerParams(
            collective_id=2, has_side_effects=True, vmem_limit_bytes=60 << 20
        ),
        name="tail",
    )(templates, weighted)


def body_by_parameters(event_bins, event_weights, nominal, background, observed):
    owners = lax.axis_size("bins")
    near = math.isqrt(owners)
    far = owners // near
    events = event_bins.shape[0]
    bins_dev = background.shape[0]
    width = event_weights.shape[1] // near
    chunks = width // LANES
    capacity = 3 * events // (2 * owners)
    slot = -(-capacity // 16) * 16 + 16
    ahead = min(-(-near * capacity // 16) * 16 + 16, events - 16)
    here = lax.axis_index("bins")
    z, me = here // near, lax.rem(here, near)
    around = [[(s, s // near * near + (s % near ^ d)) for s in range(owners)] for d in range(near)]

    def spread(value):
        return [value] + [shift(value, around[d]) for d in range(1, near)]

    firsts = []
    first_row = jnp.where(z < far // 2, events - ahead, 0)
    for d in range(near):
        corner = (first_row, (me ^ d) * width)
        firsts.append(lax.dynamic_slice(event_weights, corner, (ahead, LANES)))
    event_bins, firsts = lax.optimization_barrier((event_bins, firsts))
    for d in range(1, near):
        firsts[d] = shift(firsts[d], around[d])

    marks = jnp.arange(owners, dtype=jnp.int32) * bins_dev
    before = jnp.sum((event_bins[None, :] < marks[:, None]).astype(jnp.int32), axis=1)
    starts = jnp.minimum(before // 16, (events - slot) // 16)
    places = slots_of(starts, event_bins, nominal, slot, bins_dev)
    places = jnp.stack(spread(places))

    starts = places[:, 2 * owners, :owners].astype(jnp.int32).reshape(-1)
    places = places[:, : 2 * owners].transpose(1, 0, 2).reshape(2 * owners, 1, near * slot)
    worth = places[owners:]
    places = places[:owners].astype(jnp.int32)
    data = jnp.concatenate([background, observed]).reshape(-1, LANES)
    templates, weighted = chain(
        starts, places, worth, data, event_weights, firsts, near, far, chunks, slot, bins_dev
    )
    summed = tail(templates, weighted, near, far)
    return summed * (1.0 / (bins_dev * owners))


def splits_by_parameters(mesh, event_bins, event_weights, background):
    owners, groups = mesh.shape["bins"], mesh.shape["params"]
    near = math.isqrt(owners)
    events = event_bins.shape[0] // owners
    width = event_weights.shape[1] // groups // max(near, 1)
    bins_dev = background.shape[0] // owners
    return (
        groups == 2
        and near == 4
        and near * near == owners
        and near & (near - 1) == 0
        and width % LANES == 0
        and width % (16 * near) == 0
        and events % LANES == 0
        and events >= 2 * LANES
        and bins_dev % (8 * LANES) == 0
    )


def solution(mesh):
    in_specs = (P("bins"), P("bins", "params"), P("bins"), P("bins"), P("bins"))
    out_specs = P(("params", "bins"), None)

    def run(event_bins, event_weights, nominal, background, observed):
        fits = splits_by_parameters(mesh, event_bins, event_weights, background)
        chosen = body_by_parameters if fits else body
        mapped = jax.shard_map(
            chosen, mesh=mesh, in_specs=in_specs, out_specs=out_specs, check_vma=False
        )
        return mapped(event_bins, event_weights, nominal, background, observed)

    return run
```

profile of v0, /device:TPU:28, one launch (start us, length us, event | category | flops | bytes accessed | tf_op | source)
XLA Modules:
  0.0 320.7 jit_solution(7655599376472400886)
XLA Ops:
  0.0 1.3 reshape.31.nominal_ref
  1.3 2.1 fusion.3
  3.4 0.2 convert_reduce_fusion
  3.6 0.6 fusion.2.starts_ref
  4.2 3.3 %slots.1 = f32[33,304]{1,0:T(8,128)} custom-call(s32[16]{0:T(128)} %fusion.2.starts_ref, s32[1,3072]{1,0:T(1,128)} %bitcast.17, bf16[1,3072]{1,0:T(2,128)(2,1)} %reshape.31.nominal_ref), custom_call_target="tpu_custom_call" | custom-call | tf_op jit(solution)/shard_map/slots/pallas_call | solution.py:353
  7.4 1.4 collective-permute-start.2
  8.9 1.5 collective-permute-start.1
  10.4 0.5 collective-permute-start
  10.9 1.5 collective-permute-start.3
  12.4 0.5 collective-permute-start.4
  12.9 0.6 pad_maximum_fusion.3.data_ref
  13.5 1.5 collective-permute-start.5
  15.0 0.5 collective-permute-done
  15.5 0.7 fusion.1
  16.2 0.6 convert_element_type.17.starts_ref
  16.8 0.8 fusion
  17.7 0.8 slice.20.worth_ref
  18.5 0.8 convert_element_type.19.local_ref
  19.3 2.5 collective-permute-done.3.refs_1_
  21.9 5.0 %collective-permute-done.5.refs_3_ = bf16[1168,128]{1,0:T(8,128)(2,1)S(1)} collective-permute-done((bf16[1168,128]{1,0:T(8,128)(2,1)S(1)}, bf16[1168,128]{1,0:T(8,128)(2,1)S(1)}, u32[]{:S(2)}, u32[]{:S(2)}) %collective-permute-start.5) | collective-permute-done | bytes 299040 | tf_op jit(solution)/shard_map/ppermute | solution.py:315
  26.9 0.7 copy-done.2
  27.6 237.8 %chain.1 = (bf16[2,4,3,4096,128]{4,3,2,1,0:T(8,128)(2,1)}, bf16[384,4096]{1,0:T(8,128)(2,1)}) custom-call(s32[64]{0:T(128)} %convert_element_type.17.starts_ref, s32[16,1,1216]{2,1,0:T(1,128)} %convert_element_type.19.local_ref, f32[16,1,1216]{2,1,0:T(1,128)} %slice.20.worth_ref, f32[16,128]{1,0:T(8,128)} %pad_maximum_fusion.3.data_ref, ...), custom_call_target="tpu_custom_call" | custom-call | tf_op jit(solution)/shard_map/chain/pallas_call | solution.py:808
  265.5 52.8 %tail.1 = f32[96,3072]{1,0:T(8,128)} custom-call(bf16[2,4,3,4096,128]{4,3,2,1,0:T(8,128)(2,1)} %get-tuple-element.17.templates_ref, bf16[384,4096]{1,0:T(8,128)(2,1)} %get-tuple-element.18.weighted), custom_call_target="tpu_custom_call" | custom-call | tf_op jit(solution)/shard_map/tail/pallas_call | solution.py:1005
  318.3 2.4 broadcast_multiply_fusion
  (18 shorter events, 0.1 us)
Async XLA Ops:
  1.3 2.1 copy-start.3
  1.3 11.6 %copy-start.4 = (f32[1024]{0:T(1024)S(1)}, f32[1024]{0:T(1024)}, u32[]{:S(2)}) copy-start(f32[1024]{0:T(1024)} %param.9) | copy-start | bytes 12292
  1.3 11.6 %copy-start.5 = (f32[1024]{0:T(1024)S(1)}, f32[1024]{0:T(1024)}, u32[]{:S(2)}) copy-start(f32[1024]{0:T(1024)} %param.8) | copy-start | bytes 12292
  7.4 6.1 %collective-permute-start.2 = (f32[33,304]{1,0:T(8,128)}, f32[33,304]{1,0:T(8,128)S(1)}, u32[]{:S(2)}, u32[]{:S(2)}) collective-permute-start(f32[33,304]{1,0:T(8,128)} %slots.1), channel_id=1, source_target_pairs={{0,6},{2,4},{4,2},{6,0},{8,14},{10,12},{12,10},{14,8},{16,22},{18,... | collective-permute-start | bytes 120392 | tf_op jit(solution)/shard_map/ppermute | solution.py:315
  8.9 6.2 %collective-permute-start.1 = (f32[33,304]{1,0:T(8,128)}, f32[33,304]{1,0:T(8,128)S(1)}, u32[]{:S(2)}, u32[]{:S(2)}) collective-permute-start(f32[33,304]{1,0:T(8,128)} %slots.1), channel_id=1, source_target_pairs={{0,4},{2,6},{4,0},{6,2},{8,12},{10,14},{12,8},{14,10},{16,20},{18,... | collective-permute-start | bytes 120392 | tf_op jit(solution)/shard_map/ppermute | solution.py:315
  10.4 5.1 %collective-permute-start = (f32[33,304]{1,0:T(8,128)}, f32[33,304]{1,0:T(8,128)S(1)}, u32[]{:S(2)}, u32[]{:S(2)}) collective-permute-start(f32[33,304]{1,0:T(8,128)} %slots.1), channel_id=1, source_target_pairs={{0,2},{2,0},{4,6},{6,4},{8,10},{10,8},{12,14},{14,12},{16,18},{18,... | collective-permute-start | bytes 120392 | tf_op jit(solution)/shard_map/ppermute | solution.py:315
  10.9 11.0 %collective-permute-start.3 = (bf16[1168,128]{1,0:T(8,128)(2,1)S(1)}, bf16[1168,128]{1,0:T(8,128)(2,1)S(1)}, u32[]{:S(2)}, u32[]{:S(2)}) collective-permute-start(bf16[1168,128]{1,0:T(8,128)(2,1)S(1)} %get-tuple-element.14), channel_id=1, source_target_pairs={{0,2},{2,0},{4,6},{6,4},{8,10},{10,8},{12,14},{14,12},{16,18},{18,... | collective-permute-start | bytes 897032 | tf_op jit(solution)/shard_map/ppermute | solution.py:315
  12.4 9.5 %collective-permute-start.4 = (bf16[1168,128]{1,0:T(8,128)(2,1)S(1)}, bf16[1168,128]{1,0:T(8,128)(2,1)S(1)}, u32[]{:S(2)}, u32[]{:S(2)}) collective-permute-start(bf16[1168,128]{1,0:T(8,128)(2,1)S(1)} %get-tuple-element.15), channel_id=1, source_target_pairs={{0,4},{2,6},{4,0},{6,2},{8,12},{10,14},{12,8},{14,10},{16,20},{18,... | collective-permute-start | bytes 897032 | tf_op jit(solution)/shard_map/ppermute | solution.py:315
  13.5 13.4 %collective-permute-start.5 = (bf16[1168,128]{1,0:T(8,128)(2,1)S(1)}, bf16[1168,128]{1,0:T(8,128)(2,1)S(1)}, u32[]{:S(2)}, u32[]{:S(2)}) collective-permute-start(bf16[1168,128]{1,0:T(8,128)(2,1)S(1)} %get-tuple-element.16), channel_id=1, source_target_pairs={{0,6},{2,4},{4,2},{6,0},{8,14},{10,12},{12,10},{14,8},{16,22},{18,... | collective-permute-start | bytes 897032 | tf_op jit(solution)/shard_map/ppermute | solution.py:315
  21.9 5.0 %copy-start = (bf16[1168,128]{1,0:T(8,128)(2,1)}, bf16[1168,128]{1,0:T(8,128)(2,1)S(1)}, u32[]{:S(2)}) copy-start(bf16[1168,128]{1,0:T(8,128)(2,1)S(1)} %collective-permute-done.3.refs_1_) | copy-start | bytes 897028
  21.9 5.0 %copy-start.1 = (bf16[1168,128]{1,0:T(8,128)(2,1)}, bf16[1168,128]{1,0:T(8,128)(2,1)S(1)}, u32[]{:S(2)}) copy-start(bf16[1168,128]{1,0:T(8,128)(2,1)S(1)} %collective-permute-done.4.refs_2_) | copy-start | bytes 897028
  26.9 0.7 copy-start.2
where the time goes:
time: 325 us; the launch traced here: 321 us
  Pallas kernels  294 us (90%)
  waiting for transfers between devices  8 us (2%)
  starting transfers between devices  6.98 us (2%)
  local copies, waits for them, and re-layouts  6.45 us (2%)
  other arithmetic  5.27 us (2%)
    pallas_call x1, Pallas kernels, chain(): pl.pallas_call(functools.partial(chain_kernel, near, far, chunks, pieces,...  238 us
    pallas_call x1, Pallas kernels, tail(): pl.pallas_call(functools.partial(tail_kernel, near, far), out_shape=jax.S...  52.8 us
    ppermute x6, waiting for transfers between devices, shift(): return lax.ppermute(value, 'bins', pairs)  8 us
    ppermute x6, starting transfers between devices, shift(): return lax.ppermute(value, 'bins', pairs)  6.98 us
  transfers between devices with their start and end apart: 6, of which 3 were waited for; matrix products, arithmetic and copies ran while one was open for 1% of the time, Pallas kernels for 0%

commit v1 on v0

--- a/solution.py
+++ b/solution.py
@@ -361,7 +361,7 @@
 
 
 def chain_kernel(
-    near, far, chunks, pieces, slot, starts_ref, local_ref, worth_ref, data_ref, weights_ref, *refs
+    near, far, chunks, pieces, slot, starts_ref, local_ref, data_ref, weights_ref, *refs
 ):
     firsts = refs[:near]
     out_ref, weighted_ref = refs[near : near + 2]
@@ -381,7 +381,7 @@
     width = chunks * LANES
     held = near // pieces
     size = held * bins_dev
-    direct = [d for d in range(1, near) if near != 4 or d != 3]
+    direct = [1, 2]
 
     def side(d):
         return z * near + xor_of(me, d, near)
@@ -477,12 +477,13 @@
     def nominal_sums():
         @pl.loop(0, owners)
         def _(o):
+            ids = local_ref[pl.ds(o, 1), :].astype(jnp.int32)
+            worth = local_ref[pl.ds(owners + o, 1), :]
+
             @pl.loop(0, bins_dev // TILE)
             def _(k):
                 bins = k * TILE + lax.broadcasted_iota(jnp.int32, (TILE, near * slot), 0)
-                total = jnp.sum(
-                    jnp.where(bins == local_ref[o], worth_ref[o], 0.0), axis=1, keepdims=True
-                )
+                total = jnp.sum(jnp.where(bins == ids, worth, 0.0), axis=1, keepdims=True)
                 for h in range(TILE // LANES):
                     part = total[h * LANES : (h + 1) * LANES]
                     line = o * (bins_dev // LANES) + k * (TILE // LANES) + h
@@ -540,10 +541,12 @@
                     part = rows_refs[c][s, pl.ds(start * 16, slot), :]
                 window[s * slot : (s + 1) * slot, :] = part
 
+            ids = local_ref[pl.ds(owner, 1), :].astype(jnp.int32)
+
             @pl.loop(0, bins_dev // TILE)
             def _(k):
                 bins = k * TILE + lax.broadcasted_iota(jnp.int32, (TILE, near * slot), 0)
-                hot = (bins == local_ref[owner]).astype(jnp.bfloat16)
+                hot = (bins == ids).astype(jnp.bfloat16)
                 acc[...] = jnp.dot(hot, window[...], preferred_element_type=jnp.float32)
                 base = i * (bins_dev // LANES) + k * (TILE // LANES)
                 eye = diagonal()
@@ -655,15 +658,26 @@
         pair_copy(c, 0, p).start()
         keep_copy(c, p).start()
 
-    def forward(c, p, act):
-        if near == 4:
-            @pl.when(lax.rem(p, 2) == 0)
-            def _():
-                act(side_copy(c, 3, p, 1, 2))
-
-            @pl.when(lax.rem(p, 2) == 1)
-            def _():
-                act(side_copy(c, 3, p, 2, 1))
+    def forward(c, p):
+        copies = []
+        for half, (source, hop, sem) in enumerate(((1, 2, 3), (2, 1, 0))):
+            part = pl.ds(pl.multiple_of(p * size + half * (size // 2), size // 2), size // 2)
+            copies.append(
+                pltpu.make_async_remote_copy(
+                    src_ref=out_ref.at[0, source, c, part, :],
+                    dst_ref=out_ref.at[0, 3, c, part, :],
+                    send_sem=side_send.at[c, sem, p],
+                    recv_sem=side_recv.at[c, sem, p],
+                    device_id={"bins": side(hop)},
+                    device_id_type=MESH,
+                )
+            )
+        return copies
+
+    def stage_copy(c, d, p):
+        return pltpu.make_async_copy(
+            out_ref.at[0, d, c, rows_part(p), :], stage.at[p, d - 1], stage_sem.at[p, d - 1]
+        )
 
     def over(c, span, act):
         @pl.loop(span[0], span[1])
@@ -673,24 +687,18 @@
     def relay(c, p):
         for d in direct:
             side_copy(c, d, p).wait_recv()
-        forward(c, p, lambda copy: copy.start())
+        for copy in forward(c, p):
+            copy.start()
         for d in direct:
             pair_copy(c, d, p).start()
 
     def relay_last(c, p):
-        for d in range(1, near):
-            if d not in direct:
-                side_copy(c, d, p).wait_recv()
-                pair_copy(c, d, p).start()
-
-    def stage_copy(c, d, p):
-        return pltpu.make_async_copy(
-            out_ref.at[0, d, c, rows_part(p), :], stage.at[p, d - 1], stage_sem.at[p, d - 1]
-        )
-
-    def fetch(c, p):
-        for d in range(1, near):
+        for d in direct:
             stage_copy(c, d, p).start()
+        for copy in forward(c, p):
+            copy.wait_recv()
+        stage_copy(c, 3, p).start()
+        pair_copy(c, 3, p).start()
 
     def weigh(c, p):
         for d in range(1, near):
@@ -729,7 +737,6 @@
 
     def weigh_all(c, span):
         over(c, span, relay_last)
-        over(c, span, fetch)
         over(c, span, weigh)
 
     every = (0, pieces)
@@ -778,7 +785,8 @@
             keep_copy(c, p).wait()
             for d in direct:
                 side_copy(c, d, p).wait_send()
-            forward(c, p, lambda copy: copy.wait_send())
+            for copy in forward(c, p):
+                copy.wait_send()
             for d in range(near):
                 pair_copy(c, d, p).wait_send()
                 pair_copy(c, d, p).wait_recv()
@@ -794,7 +802,7 @@
                             copy.wait_send()
 
 
-def chain(starts, local, worth, data, weights, firsts, near, far, chunks, slot, bins_dev):
+def chain(starts, local, data, weights, firsts, near, far, chunks, slot, bins_dev):
     events = weights.shape[0]
     ahead = firsts[0].shape[0]
     pieces = near
@@ -812,7 +820,7 @@
             jax.ShapeDtypeStruct((chunks * LANES * near // far, bins), rows),
         ],
         in_specs=[pl.BlockSpec(memory_space=pltpu.SMEM)]
-        + [pl.BlockSpec(memory_space=pltpu.VMEM)] * 3
+        + [pl.BlockSpec(memory_space=pltpu.VMEM)] * 2
         + [pl.BlockSpec(memory_space=pl.ANY)] * (1 + near),
         out_specs=[
             pl.BlockSpec(memory_space=pl.ANY),
@@ -858,7 +866,7 @@
             collective_id=3, has_side_effects=True, vmem_limit_bytes=62 << 20
         ),
         name="chain",
-    )(starts, local, worth, data, weights, *firsts)
+    )(starts, local, data, weights, *firsts)
 
 
 def tail_kernel(
@@ -1062,12 +1070,10 @@
     places = jnp.stack(spread(places))
 
     starts = places[:, 2 * owners, :owners].astype(jnp.int32).reshape(-1)
-    places = places[:, : 2 * owners].transpose(1, 0, 2).reshape(2 * owners, 1, near * slot)
-    worth = places[owners:]
-    places = places[:owners].astype(jnp.int32)
+    places = places.transpose(1, 0, 2).reshape(2 * owners + 1, near * slot)
     data = jnp.concatenate([background, observed]).reshape(-1, LANES)
     templates, weighted = chain(
-        starts, places, worth, data, event_weights, firsts, near, far, chunks, slot, bins_dev
+        starts, places, data, event_weights, firsts, near, far, chunks, slot, bins_dev
     )
     summed = tail(templates, weighted, near, far)
     return summed * (1.0 / (bins_dev * owners))

time: 325 us -> 324 us (level)
  transfers between devices with their start and end apart: 6 -> 6, of which waited for: 3 -> 4; matrix products, arithmetic and copies ran while one was open for 1% -> 1% of each run, Pallas kernels for 0% -> 0%
where the time goes in v1:
time: 324 us; the launch traced here: 319 us
  Pallas kernels  293 us (90%)
  waiting for transfers between devices  9.52 us (3%)
  starting transfers between devices  6.86 us (2%)
  local copies, waits for them, and re-layouts  5.7 us (2%)
  other arithmetic  4.62 us (1%)
    pallas_call x1, Pallas kernels, chain(): pl.pallas_call(functools.partial(chain_kernel, near, far, chunks, pieces,...  236 us
    pallas_call x1, Pallas kernels, tail(): pl.pallas_call(functools.partial(tail_kernel, near, far), out_shape=jax.S...  53.6 us
    ppermute x6, waiting for transfers between devices, shift(): return lax.ppermute(value, 'bins', pairs)  9.52 us
    ppermute x6, starting transfers between devices, shift(): return lax.ppermute(value, 'bins', pairs)  6.86 us
  transfers between devices with their start and end apart: 6, of which 4 were waited for; matrix products, arithmetic and copies ran while one was open for 1% of the time, Pallas kernels for 0%

profile of v1, /device:TPU:28, one launch (start us, length us, event | category | flops | bytes accessed | tf_op | source)
XLA Modules:
  0.0 319.3 jit_solution(17097330380459407883)
XLA Ops:
  0.0 1.3 reshape.18.nominal_ref
  1.3 2.1 fusion.3
  3.4 0.2 convert_reduce_fusion
  3.6 0.6 fusion.1.starts_ref
  4.2 3.3 %slots.1 = f32[33,304]{1,0:T(8,128)} custom-call(s32[16]{0:T(128)} %fusion.1.starts_ref, s32[1,3072]{1,0:T(1,128)} %bitcast.13, bf16[1,3072]{1,0:T(2,128)(2,1)} %reshape.18.nominal_ref), custom_call_target="tpu_custom_call" | custom-call | tf_op jit(solution)/shard_map/slots/pallas_call | solution.py:353
  7.4 1.4 collective-permute-start.2
  8.9 1.5 collective-permute-start.1
  10.4 0.5 collective-permute-start
  10.9 1.5 collective-permute-start.3
  12.4 0.5 collective-permute-start.4
  12.9 0.2 collective-permute-done.2
  13.1 1.4 collective-permute-start.5
  14.5 0.6 pad_maximum_fusion.1.data_ref
  15.1 0.4 collective-permute-done
  15.5 0.9 fusion.2
  16.3 0.1 copy.7
  16.4 0.8 reshape.19.local_ref
  17.3 0.7 convert_element_type.12.starts_ref
  17.9 3.9 %collective-permute-done.3.refs_1_ = bf16[1168,128]{1,0:T(8,128)(2,1)S(1)} collective-permute-done((bf16[1168,128]{1,0:T(8,128)(2,1)S(1)}, bf16[1168,128]{1,0:T(8,128)(2,1)S(1)}, u32[]{:S(2)}, u32[]{:S(2)}) %collective-permute-start.3) | collective-permute-done | bytes 299040 | tf_op jit(solution)/shard_map/ppermute | solution.py:315
  21.9 5.0 %collective-permute-done.5.refs_3_ = bf16[1168,128]{1,0:T(8,128)(2,1)S(1)} collective-permute-done((bf16[1168,128]{1,0:T(8,128)(2,1)S(1)}, bf16[1168,128]{1,0:T(8,128)(2,1)S(1)}, u32[]{:S(2)}, u32[]{:S(2)}) %collective-permute-start.5) | collective-permute-done | bytes 299040 | tf_op jit(solution)/shard_map/ppermute | solution.py:315
  26.9 0.7 copy-done.2
  27.6 235.6 %chain.1 = (bf16[2,4,3,4096,128]{4,3,2,1,0:T(8,128)(2,1)}, bf16[384,4096]{1,0:T(8,128)(2,1)}) custom-call(s32[64]{0:T(128)} %convert_element_type.12.starts_ref, f32[33,1216]{1,0:T(8,128)} %reshape.19.local_ref, f32[16,128]{1,0:T(8,128)} %pad_maximum_fusion.1.data_ref, bf16[3072,1536]{1,0:T(8,128)(2,1)} %weights_ref.1, ...), custom_call_target="tpu_custom_call" | custom-call | tf_op jit(solution)/shard_map/chain/pallas_call | solution.py:816
  263.3 53.6 %tail.1 = f32[96,3072]{1,0:T(8,128)} custom-call(bf16[2,4,3,4096,128]{4,3,2,1,0:T(8,128)(2,1)} %get-tuple-element.17.templates_ref, bf16[384,4096]{1,0:T(8,128)(2,1)} %get-tuple-element.18.weighted), custom_call_target="tpu_custom_call" | custom-call | tf_op jit(solution)/shard_map/tail/pallas_call | solution.py:1013
  316.9 2.4 broadcast_multiply_fusion
  (15 shorter events, 0.0 us)
Async XLA Ops:
  1.3 2.1 copy-start.3
  1.3 13.2 %copy-start.4 = (f32[1024]{0:T(1024)S(1)}, f32[1024]{0:T(1024)}, u32[]{:S(2)}) copy-start(f32[1024]{0:T(1024)} %param.9) | copy-start | bytes 12292
  1.3 13.2 %copy-start.5 = (f32[1024]{0:T(1024)S(1)}, f32[1024]{0:T(1024)}, u32[]{:S(2)}) copy-start(f32[1024]{0:T(1024)} %param.8) | copy-start | bytes 12292
  7.4 5.7 %collective-permute-start.2 = (f32[33,304]{1,0:T(8,128)}, f32[33,304]{1,0:T(8,128)S(1)}, u32[]{:S(2)}, u32[]{:S(2)}) collective-permute-start(f32[33,304]{1,0:T(8,128)} %slots.1), channel_id=1, source_target_pairs={{0,6},{2,4},{4,2},{6,0},{8,14},{10,12},{12,10},{14,8},{16,22},{18,... | collective-permute-start | bytes 120392 | tf_op jit(solution)/shard_map/ppermute | solution.py:315
  8.9 6.2 %collective-permute-start.1 = (f32[33,304]{1,0:T(8,128)}, f32[33,304]{1,0:T(8,128)S(1)}, u32[]{:S(2)}, u32[]{:S(2)}) collective-permute-start(f32[33,304]{1,0:T(8,128)} %slots.1), channel_id=1, source_target_pairs={{0,4},{2,6},{4,0},{6,2},{8,12},{10,14},{12,8},{14,10},{16,20},{18,... | collective-permute-start | bytes 120392 | tf_op jit(solution)/shard_map/ppermute | solution.py:315
  10.4 5.1 %collective-permute-start = (f32[33,304]{1,0:T(8,128)}, f32[33,304]{1,0:T(8,128)S(1)}, u32[]{:S(2)}, u32[]{:S(2)}) collective-permute-start(f32[33,304]{1,0:T(8,128)} %slots.1), channel_id=1, source_target_pairs={{0,2},{2,0},{4,6},{6,4},{8,10},{10,8},{12,14},{14,12},{16,18},{18,... | collective-permute-start | bytes 120392 | tf_op jit(solution)/shard_map/ppermute | solution.py:315
  10.9 11.0 %collective-permute-start.3 = (bf16[1168,128]{1,0:T(8,128)(2,1)S(1)}, bf16[1168,128]{1,0:T(8,128)(2,1)S(1)}, u32[]{:S(2)}, u32[]{:S(2)}) collective-permute-start(bf16[1168,128]{1,0:T(8,128)(2,1)S(1)} %get-tuple-element.14), channel_id=1, source_target_pairs={{0,2},{2,0},{4,6},{6,4},{8,10},{10,8},{12,14},{14,12},{16,18},{18,... | collective-permute-start | bytes 897032 | tf_op jit(solution)/shard_map/ppermute | solution.py:315
  12.4 9.5 %collective-permute-start.4 = (bf16[1168,128]{1,0:T(8,128)(2,1)S(1)}, bf16[1168,128]{1,0:T(8,128)(2,1)S(1)}, u32[]{:S(2)}, u32[]{:S(2)}) collective-permute-start(bf16[1168,128]{1,0:T(8,128)(2,1)S(1)} %get-tuple-element.15), channel_id=1, source_target_pairs={{0,4},{2,6},{4,0},{6,2},{8,12},{10,14},{12,8},{14,10},{16,20},{18,... | collective-permute-start | bytes 897032 | tf_op jit(solution)/shard_map/ppermute | solution.py:315
  13.1 13.8 %collective-permute-start.5 = (bf16[1168,128]{1,0:T(8,128)(2,1)S(1)}, bf16[1168,128]{1,0:T(8,128)(2,1)S(1)}, u32[]{:S(2)}, u32[]{:S(2)}) collective-permute-start(bf16[1168,128]{1,0:T(8,128)(2,1)S(1)} %get-tuple-element.16), channel_id=1, source_target_pairs={{0,6},{2,4},{4,2},{6,0},{8,14},{10,12},{12,10},{14,8},{16,22},{18,... | collective-permute-start | bytes 897032 | tf_op jit(solution)/shard_map/ppermute | solution.py:315
  21.9 5.0 %copy-start = (bf16[1168,128]{1,0:T(8,128)(2,1)}, bf16[1168,128]{1,0:T(8,128)(2,1)S(1)}, u32[]{:S(2)}) copy-start(bf16[1168,128]{1,0:T(8,128)(2,1)S(1)} %collective-permute-done.3.refs_1_) | copy-start | bytes 897028
  21.9 5.0 %copy-start.1 = (bf16[1168,128]{1,0:T(8,128)(2,1)}, bf16[1168,128]{1,0:T(8,128)(2,1)S(1)}, u32[]{:S(2)}) copy-start(bf16[1168,128]{1,0:T(8,128)(2,1)S(1)} %collective-permute-done.4.refs_2_) | copy-start | bytes 897028
  26.9 0.7 copy-start.2
